TPU v7x, 32 devices: a whole 2x2x4 slice. The times are simulated.
32 devices in a mesh: groups: 2 (over y), text: 4 (over z), image: 4 (over x, core).
Axes of the slice: x: 2, y: 2, z: 4, core: 2. Of those that a mesh axis runs over, the one named last changes fastest.
Arguments:
- text_states: bfloat16 [1024, 8192], P(('groups', 'text')), parts along dimension 0, may hold values from -6 to 6
- grid_levels: bfloat16 [16384, 8192], P(('groups', 'text'), 'image'), parts along dimension 0, may hold values from -8 to 7, as said below
- round_logits: float32 [16384, 8192], P(('groups', 'text'), 'image'), parts along dimension 0, may hold values from -2 to 2
- column_steps: float32 [16384], P(('groups', 'image')), parts along dimension 0, may hold values from 0.0015 to 0.004
- image_keys: bfloat16 [12808, 1024], P('groups', 'image'), parts along dimension 0, may hold values from -500 to 500
- image_values: bfloat16 [12808, 1024], P('groups', 'image'), parts along dimension 0, may hold values from -6 to 6
- target_out: bfloat16 [1024, 8192], P(('groups', 'text'), 'image'), parts along dimension 0, may hold values from -6 to 6
- doc_images: int32 [6], P('groups'), parts along dimension 0, may hold values from 1 to 2, as said below
- image_start: int32 [8], P('groups'), parts along dimension 0, may hold values from 1 to 3, as said below
Outputs:
- rounding_grad: float32 [16384, 8192], P(('groups', 'text'), 'image'), parts along dimension 0
There are 2 independent parts, one for each index of `groups`. A program takes and returns all parts, laid end to end along the dimension named above; each array names one. Nothing has to cross between parts.
Inputs may be any that keep to these rules, and one draw needn't show every extreme that they name: `doc_images`: every document holds one image or more, 4 in all; one document holds exactly 2, and no document more. `image_start`: Nondecreasing; the first image's entry is 1 and the last image's 4 - 1. `grid_levels`: whole numbers.
All inputs are finite; a program needn't handle non-finite values.
Results may differ from a plain program's by a relative error of at most 0.015.
Values may be sent and summed in bfloat16 or wider, within the bound.
A program may use at most 256 MiB of HBM per device.

v0:
```python
import jax
import jax.numpy as jnp
from jax import lax
from jax.sharding import PartitionSpec as P

H = 64
KVH = 8
HD = 128
IMAGES = 4
IMG_TOK = 1601
SPAN = 128


def visibility(span_ids, doc_images, image_start, total_spans):
    images = image_start.shape[0]
    documents = doc_images.shape[0]
    doc_ends = jnp.cumsum(doc_images)
    positions = jnp.arange(images, dtype=jnp.int32)
    doc_of = jnp.sum((positions[:, None] >= doc_ends[None, :]).astype(jnp.int32), axis=1)
    doc_index = jnp.arange(documents, dtype=jnp.int32)
    end_of = jnp.sum(jnp.where(doc_index[None, :] == doc_of[:, None], doc_ends[None, :], 0), axis=1)
    stop_at = jnp.sum(
        jnp.where(positions[None, :] == end_of[:, None], image_start[None, :], 0), axis=1
    )
    stop_at = stop_at + jnp.where(end_of >= images, total_spans, 0)
    return (span_ids[:, None] >= image_start[None, :]) & (span_ids[:, None] < stop_at[None, :])


def head_grad(queries, keys, values, target, visible):
    tokens_here = queries.shape[0]
    kv_heads = queries.shape[1]
    per_group = queries.shape[2]
    head_size = queries.shape[3]
    scaling = head_size ** (-0.5)
    shape = (kv_heads, per_group, tokens_here)

    def tile_of(which):
        keys_now = lax.dynamic_slice_in_dim(keys, which * IMG_TOK, IMG_TOK, 0)
        values_now = lax.dynamic_slice_in_dim(values, which * IMG_TOK, IMG_TOK, 0)
        scores = (
            jnp.einsum("tkgd,nkd->kgtn", queries, keys_now, preferred_element_type=jnp.float32)
            * scaling
        )
        return (scores, keys_now, values_now)

    def seen_of(which):
        return lax.dynamic_index_in_dim(visible, which, 1, keepdims=False)

    def forward(which, state):
        seen_rows = seen_of(which)
        running, total, accum = state
        scores, keys_now, values_now = tile_of(which)
        seen = seen_rows[None, None, :]
        peak = jnp.where(seen, jnp.maximum(running, jnp.max(scores, axis=-1)), running)
        weights = jnp.where(seen[..., None], jnp.exp(scores - peak[..., None]), 0.0)
        fade = jnp.exp(running - peak)
        total = total * fade + jnp.sum(weights, axis=-1)
        product = jnp.einsum(
            "kgtn,nkd->kgtd",
            weights.astype(jnp.bfloat16),
            values_now,
            preferred_element_type=jnp.float32,
        )
        return (peak, total, accum * fade[..., None] + product)

    start_state = (
        jnp.full(shape, -1e30, jnp.float32),
        jnp.zeros(shape, jnp.float32),
        jnp.zeros(shape + (head_size,), jnp.float32),
    )
    running, total, accum = lax.fori_loop(0, IMAGES, forward, start_state)
    denom = jnp.maximum(total, 1.0)
    attended = accum / denom[..., None]
    out_grad = (1024.0 * (attended - target)).astype(jnp.bfloat16)
    delta = jnp.sum(out_grad.astype(jnp.float32) * attended, axis=-1)

    def backward(which, grad_acc):
        seen_rows = seen_of(which)
        scores, keys_now, values_now = tile_of(which)
        seen = seen_rows[None, None, :]
        probs = (
            jnp.where(seen[..., None], jnp.exp(scores - running[..., None]), 0.0) / denom[..., None]
        )
        dprob = jnp.einsum(
            "kgtd,nkd->kgtn", out_grad, values_now, preferred_element_type=jnp.float32
        )
        score_grad = (probs * (dprob - delta[..., None]) * scaling).astype(jnp.bfloat16)
        return grad_acc + jnp.einsum(
            "kgtn,nkd->kgtd", score_grad, keys_now, preferred_element_type=jnp.float32
        )

    grad_sum = lax.fori_loop(0, IMAGES, backward, jnp.zeros(shape + (head_size,), jnp.float32))
    return grad_sum.astype(jnp.bfloat16)


def per_device(
    text_states,
    grid_levels,
    round_logits,
    column_steps,
    image_keys,
    image_values,
    target_out,
    doc_images,
    image_start,
):
    tok_dev = text_states.shape[0]
    out_cols = grid_levels.shape[1]
    n_text = lax.axis_size("text")
    per_group = H // KVH
    kvh_dev = image_keys.shape[1] // HD
    sigmoid_v = jax.nn.sigmoid(round_logits)
    soft = 1.2 * sigmoid_v - 0.1
    weight_q = (column_steps[None, :] * (grid_levels.astype(jnp.float32) + soft)).astype(
        jnp.bfloat16
    )
    spread = lax.all_to_all(text_states, "text", split_axis=1, concat_axis=0, tiled=True)
    q_sum = jnp.dot(
        text_states,
        lax.all_gather(weight_q, "text", axis=0, tiled=True),
        preferred_element_type=jnp.float32,
    )
    queries = q_sum.astype(jnp.bfloat16)
    first_token = lax.axis_index("text") * tok_dev
    span_ids = (first_token + jnp.arange(tok_dev, dtype=jnp.int32)) // SPAN
    visible = visibility(span_ids, doc_images, image_start, n_text * tok_dev // SPAN)
    query_tiles = queries.reshape(tok_dev, kvh_dev, per_group, HD)
    key_tiles = image_keys.reshape(image_keys.shape[0], kvh_dev, HD)
    value_tiles = image_values.reshape(image_values.shape[0], kvh_dev, HD)
    target_tiles = (
        target_out.astype(jnp.float32)
        .reshape(tok_dev, kvh_dev, per_group, HD)
        .transpose(1, 2, 0, 3)
    )
    grads = head_grad(query_tiles, key_tiles, value_tiles, target_tiles, visible)
    query_grad = grads.transpose(2, 0, 1, 3).reshape(tok_dev, out_cols)
    weight_grad = lax.dot_general(
        spread,
        lax.all_gather(query_grad, "text", axis=0, tiled=True),
        (((0,), (0,)), ((), ())),
        preferred_element_type=jnp.float32,
    )
    hprime = 1.2 * sigmoid_v * (1.0 - sigmoid_v)
    centered = 2.0 * soft - 1.0
    return (weight_grad * column_steps[None, :] - 4.0 * centered * centered * centered) * hprime


def solution(mesh):
    placed = (
        P(("groups", "text"), None),
        P(("groups", "text"), "image"),
        P(("groups", "text"), "image"),
        P(("groups", "image")),
        P("groups", "image"),
        P("groups", "image"),
        P(("groups", "text"), "image"),
        P("groups"),
        P("groups"),
    )
    return jax.shard_map(
        per_device,
        mesh=mesh,
        in_specs=placed,
        out_specs=P(("groups", "text"), "image"),
        check_vma=False,
    )
```

profile of v0, /device:TPU:0, one launch (start us, length us, event | category | flops | bytes accessed | tf_op | source)
XLA Modules:
  0.0 935.5 jit_solution(14713893510451674385)
XLA Ops:
  6.5 17.6 %copy.62 = f32[2048,2048]{0,1:T(8,128)} copy(f32[2048,2048]{1,0:T(8,128)} %param.15) | data formatting | bytes 33554432 | tf_op args[2]
  24.1 12.3 %copy.61 = bf16[2048,2048]{0,1:T(8,128)(2,1)} copy(bf16[2048,2048]{1,0:T(8,128)(2,1)} %param.14) | data formatting | bytes 16777216 | tf_op args[1]
  36.4 13.9 %multiply_convert_fusion = bf16[2048,2048]{0,1:T(8,128)(2,1)} fusion(bf16[2048,2048]{0,1:T(8,128)(2,1)} %copy.61, f32[2048]{0:T(1024)S(1)} %copy-done.6, f32[2048,2048]{0,1:T(8,128)} %copy.62), kind=kLoop, calls=%fused_computation.48 | loop fusion | flops 37748736 | bytes 33562624 | tf_op jit(solution)/shard_map/convert_element_type | solution.py:114
  50.4 2.5 copy.74
  52.9 6.3 all-to-all-start
  59.4 6.1 copy.63
  65.5 6.1 copy.66
  71.6 5.8 copy.60
  77.4 5.8 copy.69
  84.1 563.4 %all-gather.3.cloned.1.call-done = bf16[8192,2048]{0,1:T(8,128)(2,1)} async-done(((bf16[2048,2048]{0,1:T(8,128)(2,1)}), bf16[8192,2048]{0,1:T(8,128)(2,1)}) %all-gather.3.cloned.1.call-update) | async-done | bytes 33554448 | tf_op jit(solution)/shard_map/all_gather | solution.py:120
  647.5 15.9 %convolution_convert_fusion = bf16[2048,128]{1,0:T(8,128)(2,1)} fusion(bf16[8192,2048]{0,1:T(8,128)(2,1)} %all-gather.3.cloned.1.call-done, bf16[128,8192]{1,0:T(8,128)(2,1)S(1)} %copy-done), kind=kOutput, calls=%fused_computation.50 | convolution fusion | flops 4295229440 | bytes 36175872 | tf_op jit(solution)/shard_map/dot_general | solution.py:118
  663.4 1.3 copy.70
  664.7 94.8 %while.32 = (s32[]{:T(128)}, f32[2,8,128]{2,1,0:T(8,128)S(1)}, f32[2,8,128]{2,1,0:T(8,128)S(1)}, f32[2,8,128,128]{3,2,1,0:T(8,128)}, pred[128,4]{0,1:T(4,128)(4,...) while((s32[]{:T(128)}, f32[2,8,128]{2,1,0:T(8,128)S(1)}, ...), condition=%wide.region_7.8_spmd.clone, body=%wide.region_4.7_spmd.clone.sunk | while | flops 1712357376 | bytes 52192112 | solution.py:71
  664.9 7.8 bitcast_reduce_fusion.2
  672.8 7.3 fusion.70
  680.1 7.5 fusion.72
  687.6 0.9 copy-done.4
  688.6 7.8 bitcast_reduce_fusion.2
  696.4 7.3 fusion.70
  703.7 7.5 fusion.72
  711.3 0.9 copy-done.4
  712.2 7.8 bitcast_reduce_fusion.2
  720.0 7.3 fusion.70
  727.4 7.5 fusion.72
  734.9 0.9 copy-done.4
  735.8 7.8 bitcast_reduce_fusion.2
  743.7 7.3 fusion.70
  751.0 7.5 fusion.72
  758.5 0.9 copy-done.4
  759.5 1.6 copy.67
  761.7 83.7 %while.33 = (s32[]{:T(128)}, f32[2,8,128,128]{3,2,1,0:T(8,128)}, pred[128,4]{0,1:T(4,128)(4,1)S(1)}, bf16[6404,2,128]{2,0,1:T(8,128)(2,1)}, bf16[128,2,8,128]{3,...) while((s32[]{:T(128)}, f32[2,8,128,128]{3,2,1,0:T(8,128)}, ...), condition=%wide.region_10.11_spmd.clone, body=%wide.region_9.10_spmd.clone.sunk | while | flops 2544910336 | bytes 40319100 | solution.py:92
  762.0 7.8 fusion.78
  769.8 12.0 %fusion.79 = f32[2,8,128,128]{3,2,1,0:T(8,128)S(1)} fusion(f32[2,1601,128,8]{2,1,3,0:T(8,128)} %fusion.78, bf16[2,8,128,128]{3,2,1,0:T(8,128)(2,1)S(1)} %get-tuple-element.701, f32[2,8,128]{2,1,0:T(8,128)S(1)} %get-tuple-element.702, f32[2,8,128]{2,1,0:T(8,128)S(1)} %get-tuple-element.699, f32[2,8,128]{2,1,0:T(8,128)S(1)} %get-tuple-element.698, ...), kind=kOutput, calls=%fused_computation.32.clone.1 | convolution fusion | flops 1705525248 | bytes 17467008 | tf_op jit(solution)/shard_map/while/body/eval_jaxpr/kgtn,nkd->kgtd/dot_general | solution.py:88
  781.8 1.0 copy-done.2
  782.8 7.8 fusion.78
  790.7 12.0 %fusion.79 = f32[2,8,128,128]{3,2,1,0:T(8,128)S(1)} fusion(f32[2,1601,128,8]{2,1,3,0:T(8,128)} %fusion.78, bf16[2,8,128,128]{3,2,1,0:T(8,128)(2,1)S(1)} %get-tuple-element.701, f32[2,8,128]{2,1,0:T(8,128)S(1)} %get-tuple-element.702, f32[2,8,128]{2,1,0:T(8,128)S(1)} %get-tuple-element.699, f32[2,8,128]{2,1,0:T(8,128)S(1)} %get-tuple-element.698, ...), kind=kOutput, calls=%fused_computation.32.clone.1 | convolution fusion | flops 1705525248 | bytes 17467008 | tf_op jit(solution)/shard_map/while/body/eval_jaxpr/kgtn,nkd->kgtd/dot_general | solution.py:88
  802.7 1.0 copy-done.2
  803.7 7.8 fusion.78
  811.5 12.0 %fusion.79 = f32[2,8,128,128]{3,2,1,0:T(8,128)S(1)} fusion(f32[2,1601,128,8]{2,1,3,0:T(8,128)} %fusion.78, bf16[2,8,128,128]{3,2,1,0:T(8,128)(2,1)S(1)} %get-tuple-element.701, f32[2,8,128]{2,1,0:T(8,128)S(1)} %get-tuple-element.702, f32[2,8,128]{2,1,0:T(8,128)S(1)} %get-tuple-element.699, f32[2,8,128]{2,1,0:T(8,128)S(1)} %get-tuple-element.698, ...), kind=kOutput, calls=%fused_computation.32.clone.1 | convolution fusion | flops 1705525248 | bytes 17467008 | tf_op jit(solution)/shard_map/while/body/eval_jaxpr/kgtn,nkd->kgtd/dot_general | solution.py:88
  823.6 1.0 copy-done.2
  824.6 7.8 fusion.78
  832.4 12.0 %fusion.79 = f32[2,8,128,128]{3,2,1,0:T(8,128)S(1)} fusion(f32[2,1601,128,8]{2,1,3,0:T(8,128)} %fusion.78, bf16[2,8,128,128]{3,2,1,0:T(8,128)(2,1)S(1)} %get-tuple-element.701, f32[2,8,128]{2,1,0:T(8,128)S(1)} %get-tuple-element.702, f32[2,8,128]{2,1,0:T(8,128)S(1)} %get-tuple-element.699, f32[2,8,128]{2,1,0:T(8,128)S(1)} %get-tuple-element.698, ...), kind=kOutput, calls=%fused_computation.32.clone.1 | convolution fusion | flops 1705525248 | bytes 17467008 | tf_op jit(solution)/shard_map/while/body/eval_jaxpr/kgtn,nkd->kgtd/dot_general | solution.py:88
  844.4 1.0 copy-done.2
  845.4 2.2 copy.73
  847.7 2.9 copy.75
  850.6 42.5 %all-gather.5.cloned.1.call-done = bf16[512,2048]{0,1:T(8,128)(2,1)} async-done(((bf16[128,2048]{0,1:T(8,128)(2,1)}), bf16[512,2048]{0,1:T(8,128)(2,1)}) %all-gather.5.cloned.1.call-update) | async-done | bytes 2097168 | tf_op jit(solution)/shard_map/all_gather | solution.py:139
  893.2 17.9 %fusion.42 = f32[2048,2048]{0,1:T(8,128)} fusion(bf16[512,2048]{0,1:T(8,128)(2,1)} %all-gather.5.cloned.1.call-done, bf16[512,2048]{1,0:T(8,128)(2,1)S(1)} %bitcast.136, f32[2048]{0:T(1024)S(1)} %copy-done.7, f32[2048,2048]{0,1:T(8,128)} %copy.62), kind=kOutput, calls=%fused_computation.47 | convolution fusion | flops 4357881856 | bytes 37756928 | tf_op jit(solution)/shard_map/dot_general | solution.py:137
  911.1 17.6 %copy.76 = f32[2048,2048]{1,0:T(8,128)} copy(f32[2048,2048]{0,1:T(8,128)} %fusion.42) | data formatting | bytes 33554432 | tf_op jit(solution)/shard_map/mul | solution.py:145
  (76 shorter events, 1.9 us)
Async XLA Ops:
  6.5 640.9 %all-gather.3.cloned.1.call-start = ((), (), s32[]{:S(2)}) async-start(), calls=%async_computation.1 | async-start | bytes 41943040 | tf_op jit(solution)/shard_map/all_gather | solution.py:120
  24.1 12.3 %copy-start.6 = (f32[2048]{0:T(1024)S(1)}, f32[2048]{0:T(1024)}, u32[]{:S(2)}) copy-start(f32[2048]{0:T(1024)} %param.16) | copy-start | bytes 24580
  36.4 14.0 %copy-start = (bf16[128,8192]{1,0:T(8,128)(2,1)S(1)}, bf16[128,8192]{1,0:T(8,128)(2,1)}, u32[]{:S(2)}) copy-start(bf16[128,8192]{1,0:T(8,128)(2,1)} %param.13) | copy-start | bytes 6291460
  50.4 8.9 copy-start.9
  52.9 794.8 %all-to-all-start = ((bf16[128,4,2048]{0,2,1:T(8,128)(2,1)}), bf16[128,4,2048]{0,2,1:T(8,128)(2,1)}, u32[]{:S(2)}, u32[]{:S(2)}) async-start(bf16[128,4,2048]{0,2,1:T(8,128)(2,1)} %bitcast.11), calls=%async_computation | async-start | bytes 4194304 | tf_op jit(solution)/shard_map/all_to_all | solution.py:117
  59.2 834.0 %all-gather.5.cloned.1.call-start = ((), (), s32[]{:S(2)}) async-start(), calls=%async_computation.2 | async-start | bytes 2621440 | tf_op jit(solution)/shard_map/all_gather | solution.py:139
  59.4 23.8 %copy-start.5 = (bf16[128,2048]{1,0:T(8,128)(2,1)S(1)}, bf16[128,2048]{1,0:T(8,128)(2,1)}, u32[]{:S(2)}) copy-start(bf16[128,2048]{1,0:T(8,128)(2,1)} %param.19) | copy-start | bytes 1572868
  59.4 24.4 %copy-start.8 = (s32[4]{0:T(128)S(1)}, s32[4]{0:T(128)}, u32[]{:S(2)}) copy-start(s32[4]{0:T(128)} %param.21) | copy-start | bytes 52
  664.9 15.2 %copy-start.3 = (f32[2,8,128,128]{3,2,1,0:T(8,128)S(1)}, f32[2,8,128,128]{3,2,1,0:T(8,128)}, u32[]{:S(2)}) copy-start(f32[2,8,128,128]{3,2,1,0:T(8,128)} %get-tuple-element.644) | copy-start | bytes 3145732 | tf_op jit(solution)/shard_map/while
  687.6 1.0 copy-start.4
  688.6 15.2 %copy-start.3 = (f32[2,8,128,128]{3,2,1,0:T(8,128)S(1)}, f32[2,8,128,128]{3,2,1,0:T(8,128)}, u32[]{:S(2)}) copy-start(f32[2,8,128,128]{3,2,1,0:T(8,128)} %get-tuple-element.644) | copy-start | bytes 3145732 | tf_op jit(solution)/shard_map/while
  711.2 1.0 copy-start.4
  712.2 15.2 %copy-start.3 = (f32[2,8,128,128]{3,2,1,0:T(8,128)S(1)}, f32[2,8,128,128]{3,2,1,0:T(8,128)}, u32[]{:S(2)}) copy-start(f32[2,8,128,128]{3,2,1,0:T(8,128)} %get-tuple-element.644) | copy-start | bytes 3145732 | tf_op jit(solution)/shard_map/while
  734.9 1.0 copy-start.4
  735.8 15.2 %copy-start.3 = (f32[2,8,128,128]{3,2,1,0:T(8,128)S(1)}, f32[2,8,128,128]{3,2,1,0:T(8,128)}, u32[]{:S(2)}) copy-start(f32[2,8,128,128]{3,2,1,0:T(8,128)} %get-tuple-element.644) | copy-start | bytes 3145732 | tf_op jit(solution)/shard_map/while
  758.5 1.0 copy-start.4
  761.7 131.5 %copy-start.7 = (f32[2048]{0:T(1024)S(1)}, f32[2048]{0:T(1024)}, u32[]{:S(2)}) copy-start(f32[2048]{0:T(1024)} %param.16) | copy-start | bytes 24580
  761.9 7.9 copy-start.1
  781.8 1.0 copy-start.2
  782.8 7.8 copy-start.1
  802.7 1.0 copy-start.2
  803.7 7.8 copy-start.1
  823.6 1.0 copy-start.2
  824.6 7.8 copy-start.1
  844.4 1.0 copy-start.2
Sparse Core Ops, SparseCore 0:
  50.5 596.9 all-gather.2
  847.8 45.3 all-gather.4
where the time goes:
time: 937 us; the launch traced here: 935 us
  waiting for transfers between devices  606 us (65%)
  matrix products  174 us (19%)
  local copies, waits for them, and re-layouts  90.2 us (10%)
  other arithmetic  44.4 us (5%)
  between operations  13.5 us (1%)
    all_gather x1, waiting for transfers between devices, per_device(): lax.all_gather(weight_q, 'text', axis=0, tiled=True)  563 us
    dot_general x8, matrix products, tile_of(): jnp.einsum('tkgd,nkd->kgtn', queries, keys_now, preferred_element_type=jn...  62.6 us
    unnamed x22, local copies, waits for them, and re-layouts  58 us
    dot_general x4, matrix products, backward(): jnp.einsum('kgtn,nkd->kgtd', score_grad, keys_now, preferred_element_type...  48.1 us
    all_gather x1, waiting for transfers between devices, per_device(): lax.all_gather(query_grad, 'text', axis=0, tiled=True)  42.5 us
    dot_general x4, matrix products, forward(): jnp.einsum('kgtn,nkd->kgtd', weights.astype(jnp.bfloat16), values_now, pr...  29.9 us
    reduce_sum x4, other arithmetic, forward(): total = total * fade + jnp.sum(weights, axis=-1)  29.2 us
  transfers between devices with their start and end apart: 3, of which 2 were waited for; matrix products, arithmetic and copies ran while one was open for 24% of the time, Pallas kernels for 0%

commit v1 on v0

--- a/solution.py
+++ b/solution.py
@@ -9,6 +9,15 @@
 IMAGES = 4
 IMG_TOK = 1601
 SPAN = 128
+
+
+def build_chains(chunk, out_dim):
+    chunk = jnp.moveaxis(chunk, 0, out_dim)
+    b_now = chunk.shape
+    tall = chunk.reshape(
+        *b_now[:out_dim], b_now[out_dim] * b_now[out_dim + 1], *b_now[out_dim + 2 :]
+    )
+    return tall
 
 
 def visibility(span_ids, doc_images, image_start, total_spans):
@@ -115,10 +124,29 @@
         jnp.bfloat16
     )
     spread = lax.all_to_all(text_states, "text", split_axis=1, concat_axis=0, tiled=True)
+
+    def try_all_circles(array_here, net_axis, along_dim):
+        size_here = jax.lax.axis_size(net_axis)
+        store = list(map(lambda ix: (ix, (ix + 1) % size_here), range(size_here)))
+        left_arr, arr_next = ([], [])
+        in_order = [(dd, tick) for tick, dd in store]
+        for dev in range(size_here - 1):
+            if dev % 2 == 0:
+                left_arr.append(
+                    jax.lax.ppermute(left_arr[-1] if left_arr else array_here, net_axis, store)
+                )
+            else:
+                arr_next.append(
+                    jax.lax.ppermute(arr_next[-1] if arr_next else array_here, net_axis, in_order)
+                )
+        opened = jnp.stack([*left_arr[::-1], array_here, *arr_next])
+        wide_out = jax.lax.axis_index(net_axis) - len(left_arr)
+        opened = opened[(jnp.arange(size_here) - wide_out) % size_here]
+        y1 = build_chains(opened, along_dim)
+        return y1
+
     q_sum = jnp.dot(
-        text_states,
-        lax.all_gather(weight_q, "text", axis=0, tiled=True),
-        preferred_element_type=jnp.float32,
+        text_states, try_all_circles(weight_q, "text", 0), preferred_element_type=jnp.float32
     )
     queries = q_sum.astype(jnp.bfloat16)
     first_token = lax.axis_index("text") * tok_dev

time: 937 us -> 1120 us (1.20)
  waiting for transfers between devices: 606 us -> 383 us
  starting transfers between devices: 6.32 us -> 187 us
  local copies, waits for them, and re-layouts: 90.2 us -> 259 us
  other arithmetic: 44.4 us -> 90.1 us
    all_gather x1 -> x0, waiting for transfers between devices: 563 us -> none  [per_device(): lax.all_gather(weight_q, 'text', axis=0, tiled=True)]
    ppermute x0 -> x3, waiting for transfers between devices: none -> 340 us  [the longest x2 340 us: try_all_circles(): jax.lax.ppermute(left_arr[-1] if left_arr else array_here, net_axis, store)]
    all_to_all x1, starting transfers between devices: 6.32 us -> 181 us  [per_device(): lax.all_to_all(text_states, 'text', split_axis=1, concat_axis=0, tiled=True)]
    gather x0 -> x65, local copies, waits for them, and re-layouts: none -> 163 us
    unnamed x4 -> x5, other arithmetic: 0.01 us -> 23 us
    another operation x1 -> x2, other arithmetic: 0.18 us -> 22.9 us  [the longest x1 22.7 us: try_all_circles(): opened = jnp.stack([*left_arr[::-1], array_here, *arr_next])]
    unnamed x22 -> x34, local copies, waits for them, and re-layouts: 58 us -> 69 us
  transfers between devices with their start and end apart: 3 -> 5, of which waited for: 2 -> 3; matrix products, arithmetic and copies ran while one was open for 24% -> 40% of each run, Pallas kernels for 0% -> 0%
where the time goes in v1:
time: 1120 us; the launch traced here: 1110 us
  waiting for transfers between devices  383 us (34%)
  local copies, waits for them, and re-layouts  259 us (23%)
  starting transfers between devices  187 us (17%)
  matrix products  175 us (16%)
  other arithmetic  90.1 us (8%)
  between operations  13.9 us (1%)
    ppermute x2, waiting for transfers between devices, try_all_circles(): jax.lax.ppermute(left_arr[-1] if left_arr else array_here, net_axis, store)  340 us
    all_to_all x1, starting transfers between devices, per_device(): lax.all_to_all(text_states, 'text', split_axis=1, concat_axis=0, tiled=True)  181 us
    gather x64, local copies, waits for them, and re-layouts  140 us
    unnamed x34, local copies, waits for them, and re-layouts  69 us
    dot_general x8, matrix products, tile_of(): jnp.einsum('tkgd,nkd->kgtn', queries, keys_now, preferred_element_type=jn...  62.6 us
    dot_general x4, matrix products, backward(): jnp.einsum('kgtn,nkd->kgtd', score_grad, keys_now, preferred_element_type...  48.1 us
    all_gather x1, waiting for transfers between devices, per_device(): lax.all_gather(query_grad, 'text', axis=0, tiled=True)  43 us
    dot_general x4, matrix products, forward(): jnp.einsum('kgtn,nkd->kgtd', weights.astype(jnp.bfloat16), values_now, pr...  29.9 us
  transfers between devices with their start and end apart: 5, of which 3 were waited for; matrix products, arithmetic and copies ran while one was open for 40% of the time, Pallas kernels for 0%

profile of v1, /device:TPU:0, one launch (start us, length us, event | category | flops | bytes accessed | tf_op | source)
XLA Modules:
  0.0 1108.5 jit_solution(2086125572232701774)
XLA Ops:
  6.5 17.6 %copy.78 = f32[2048,2048]{0,1:T(8,128)} copy(f32[2048,2048]{1,0:T(8,128)} %param.15) | data formatting | bytes 33554432 | tf_op args[2]
  24.1 12.4 %copy.77 = bf16[2048,2048]{0,1:T(8,128)(2,1)} copy(bf16[2048,2048]{1,0:T(8,128)(2,1)} %param.14) | data formatting | bytes 16777216 | tf_op args[1]
  36.5 13.9 %multiply_convert_fusion = bf16[2048,2048]{0,1:T(8,128)(2,1)} fusion(bf16[2048,2048]{0,1:T(8,128)(2,1)} %copy.77, f32[2048]{0:T(1024)S(1)} %copy-done.8, f32[2048,2048]{0,1:T(8,128)} %copy.78), kind=kLoop, calls=%fused_computation.62 | loop fusion | flops 37748736 | bytes 33562624 | tf_op jit(solution)/shard_map/convert_element_type | solution.py:123
  55.5 181.6 %collective-permute-done = bf16[2048,2048]{0,1:T(8,128)(2,1)} collective-permute-done((bf16[2048,2048]{0,1:T(8,128)(2,1)}, bf16[2048,2048]{0,1:T(8,128)(2,1)}, u32[]{:S(2)}, u32[]{:S(2)}) %collective-permute-start) | collective-permute-done | bytes 8388640 | tf_op jit(solution)/shard_map/ppermute | solution.py:136
  239.6 181.5 %all-to-all-start = ((bf16[128,4,2048]{0,2,1:T(8,128)(2,1)}), bf16[128,4,2048]{0,2,1:T(8,128)(2,1)}, u32[]{:S(2)}, u32[]{:S(2)}) async-start(bf16[128,4,2048]{0,2,1:T(8,128)(2,1)} %bitcast.16), calls=%async_computation | async-start | bytes 4194304 | tf_op jit(solution)/shard_map/all_to_all | solution.py:126
  421.6 4.3 copy.83
  429.5 4.3 copy.76
  440.1 158.5 %collective-permute-done.1 = bf16[2048,2048]{0,1:T(8,128)(2,1)} collective-permute-done((bf16[2048,2048]{0,1:T(8,128)(2,1)}, bf16[2048,2048]{0,1:T(8,128)(2,1)}, u32[]{:S(2)}, u32[]{:S(2)}) %collective-permute-start.1) | collective-permute-done | bytes 8388640 | tf_op jit(solution)/shard_map/ppermute | solution.py:136
  598.6 22.7 %pad_maximum_fusion = bf16[4,2048,2048]{1,2,0:T(8,128)(2,1)} fusion(bf16[1,2048,2048]{1,2,0:T(8,128)(2,1)} %bitcast.6, bf16[1,2048,2048]{1,2,0:T(8,128)(2,1)} %bitcast.5, bf16[1,2048,2048]{1,2,0:T(8,128)(2,1)} %bitcast.4, bf16[1,2048,2048]{1,2,0:T(8,128)(2,1)} %bitcast.3), kind=kLoop, calls=%fused_computation.57 | loop fusion | flops 50331648 | bytes 67108864 | tf_op jit(solution)/shard_map/stack | solution.py:142
  621.3 23.2 %fusion.48 = (bf16[4,512,2048]{1,2,0:T(8,128)(2,1)}, bf16[4,512,2048]{1,2,0:T(8,128)(2,1)}, bf16[4,512,2048]{1,2,0:T(8,128)(2,1)}, bf16[4,512,2048]{1,2,0:T(8,128)(2,1)}) fusion(bf16[4,2048,2048]{1,2,0:T(8,128)(2,1)} %pad_maximum_fusion), kind=kLoop, calls=%fused_computation.90 | loop fusion | bytes 67108864 | tf_op jit(solution)/shard_map/gather | solution.py:144
  644.5 4.3 broadcast.168.clone.3
  648.7 34.9 %while.36 = (s32[]{:T(128)}, bf16[4,512,2048]{1,2,0:T(8,128)(2,1)}, s32[4,1]{0,1:T(1,128)S(1)}, bf16[4,512,2048]{2,1,0:T(8,128)(2,1)}, s32[]{:T(128)}) while((s32[]{:T(128)}, bf16[4,512,2048]{1,2,0:T(8,128)(2,1)}, s32[4,1]{0,1:T(1,128)S(1)}, bf16[4,512,2048]{2,1,0:T(8,128)(2,1)}, s32[]{:T(128)}) %tuple.152), condition=%wide.while_cond, body=%wide.while_body.sunk | while | flops 2 | bytes 12583501 | solution.py:144
  649.4 3.7 constant_dynamic-slice_fusion.17
  666.9 3.7 constant_dynamic-slice_fusion.17
  675.6 3.7 constant_dynamic-slice_fusion.17
  683.7 4.3 broadcast.168.clone.2
  688.0 34.9 %while.37 = (s32[]{:T(128)}, bf16[4,512,2048]{1,2,0:T(8,128)(2,1)}, s32[4,1]{0,1:T(1,128)S(1)}, bf16[4,512,2048]{2,1,0:T(8,128)(2,1)}, s32[]{:T(128)}) while((s32[]{:T(128)}, bf16[4,512,2048]{1,2,0:T(8,128)(2,1)}, s32[4,1]{0,1:T(1,128)S(1)}, bf16[4,512,2048]{2,1,0:T(8,128)(2,1)}, s32[]{:T(128)}) %tuple.170), condition=%wide.while_cond.1, body=%wide.while_body.1.sunk | while | flops 2 | bytes 12583501 | solution.py:144
  722.9 4.3 broadcast.168.clone.1
  727.2 34.9 %while.38 = (s32[]{:T(128)}, bf16[4,512,2048]{1,2,0:T(8,128)(2,1)}, s32[4,1]{0,1:T(1,128)S(1)}, bf16[4,512,2048]{2,1,0:T(8,128)(2,1)}, s32[]{:T(128)}) while((s32[]{:T(128)}, bf16[4,512,2048]{1,2,0:T(8,128)(2,1)}, s32[4,1]{0,1:T(1,128)S(1)}, bf16[4,512,2048]{2,1,0:T(8,128)(2,1)}, s32[]{:T(128)}) %tuple.171), condition=%wide.while_cond.2, body=%wide.while_body.2.sunk | while | flops 2 | bytes 12583501 | solution.py:144
  762.1 4.3 broadcast.168.clone
  766.4 34.9 %while.39 = (s32[]{:T(128)}, bf16[4,512,2048]{1,2,0:T(8,128)(2,1)}, s32[4,1]{0,1:T(1,128)S(1)}, bf16[4,512,2048]{2,1,0:T(8,128)(2,1)}, s32[]{:T(128)}) while((s32[]{:T(128)}, bf16[4,512,2048]{1,2,0:T(8,128)(2,1)}, s32[4,1]{0,1:T(1,128)S(1)}, bf16[4,512,2048]{2,1,0:T(8,128)(2,1)}, s32[]{:T(128)}) %tuple.172), condition=%wide.while_cond.3, body=%wide.while_body.3.sunk | while | flops 2 | bytes 12583501 | solution.py:144
  801.3 23.0 %pad_maximum_fusion.1 = bf16[4,2048,2048]{2,1,0:T(8,128)(2,1)} fusion(bf16[4,512,2048]{2,1,0:T(8,128)(2,1)} %get-tuple-element.350, bf16[4,512,2048]{2,1,0:T(8,128)(2,1)} %get-tuple-element.342, bf16[4,512,2048]{2,1,0:T(8,128)(2,1)} %get-tuple-element.334, bf16[4,512,2048]{2,1,0:T(8,128)(2,1)} %get-tuple-element.326), kind=kLoop, calls=%fused_computation.58 | loop fusion | flops 134217728 | bytes 67108864
  824.3 16.5 %convolution_convert_fusion = bf16[2048,128]{1,0:T(8,128)(2,1)} fusion(bf16[8192,2048]{1,0:T(8,128)(2,1)} %bitcast.149, bf16[128,8192]{1,0:T(8,128)(2,1)S(1)} %copy-done.2), kind=kOutput, calls=%fused_computation.64 | convolution fusion | flops 4295229440 | bytes 36175872 | tf_op jit(solution)/shard_map/dot_general | solution.py:148
  842.2 90.8 %while.40 = (s32[]{:T(128)}, f32[2,8,128]{2,1,0:T(8,128)S(1)}, f32[2,8,128]{2,1,0:T(8,128)S(1)}, f32[2,8,128,128]{3,2,1,0:T(8,128)S(1)}, pred[128,4]{0,1:T(4,128...) while((s32[]{:T(128)}, f32[2,8,128]{2,1,0:T(8,128)S(1)}, ...), condition=%wide.region_7.8_spmd.clone, body=%wide.region_4.7_spmd.clone.sunk | while | flops 1712357376 | bytes 43803448 | solution.py:80
  842.2 7.8 bitcast_reduce_fusion.2
  850.1 7.3 fusion.72
  857.4 7.5 fusion.74
  864.9 7.8 bitcast_reduce_fusion.2
  872.7 7.3 fusion.72
  880.1 7.5 fusion.74
  887.6 7.8 bitcast_reduce_fusion.2
  895.4 7.3 fusion.72
  902.7 7.5 fusion.74
  910.2 7.8 bitcast_reduce_fusion.2
  918.0 7.3 fusion.72
  925.3 7.5 fusion.74
  934.1 83.5 %while.41 = (s32[]{:T(128)}, f32[2,8,128,128]{3,2,1,0:T(8,128)}, pred[128,4]{0,1:T(4,128)(4,1)S(1)}, bf16[6404,2,128]{2,0,1:T(8,128)(2,1)}, bf16[128,2,8,128]{3,...) while((s32[]{:T(128)}, f32[2,8,128,128]{3,2,1,0:T(8,128)}, ...), condition=%wide.region_10.11_spmd.clone, body=%wide.region_9.10_spmd.clone.sunk | while | flops 2544910336 | bytes 40319100 | solution.py:101
  934.1 7.9 fusion.80
  942.0 12.0 %fusion.81 = f32[2,8,128,128]{3,2,1,0:T(8,128)S(1)} fusion(f32[2,1601,128,8]{2,1,3,0:T(8,128)} %fusion.80, bf16[2,8,128,128]{3,2,1,0:T(8,128)(2,1)S(1)} %get-tuple-element.1009, f32[2,8,128]{2,1,0:T(8,128)S(1)} %get-tuple-element.1010, f32[2,8,128]{2,1,0:T(8,128)S(1)} %get-tuple-element.1007, f32[2,8,128]{2,1,0:T(8,128)S(1)} %get-tuple-element.1006, ...), kind=kOutput, calls=%fused_computation.44.clone.1 | convolution fusion | flops 1705525248 | bytes 17467008 | tf_op jit(solution)/shard_map/while/body/eval_jaxpr/kgtn,nkd->kgtd/dot_general | solution.py:97
  955.0 7.9 fusion.80
  962.8 12.0 %fusion.81 = f32[2,8,128,128]{3,2,1,0:T(8,128)S(1)} fusion(f32[2,1601,128,8]{2,1,3,0:T(8,128)} %fusion.80, bf16[2,8,128,128]{3,2,1,0:T(8,128)(2,1)S(1)} %get-tuple-element.1009, f32[2,8,128]{2,1,0:T(8,128)S(1)} %get-tuple-element.1010, f32[2,8,128]{2,1,0:T(8,128)S(1)} %get-tuple-element.1007, f32[2,8,128]{2,1,0:T(8,128)S(1)} %get-tuple-element.1006, ...), kind=kOutput, calls=%fused_computation.44.clone.1 | convolution fusion | flops 1705525248 | bytes 17467008 | tf_op jit(solution)/shard_map/while/body/eval_jaxpr/kgtn,nkd->kgtd/dot_general | solution.py:97
  975.8 7.9 fusion.80
  983.7 12.0 %fusion.81 = f32[2,8,128,128]{3,2,1,0:T(8,128)S(1)} fusion(f32[2,1601,128,8]{2,1,3,0:T(8,128)} %fusion.80, bf16[2,8,128,128]{3,2,1,0:T(8,128)(2,1)S(1)} %get-tuple-element.1009, f32[2,8,128]{2,1,0:T(8,128)S(1)} %get-tuple-element.1010, f32[2,8,128]{2,1,0:T(8,128)S(1)} %get-tuple-element.1007, f32[2,8,128]{2,1,0:T(8,128)S(1)} %get-tuple-element.1006, ...), kind=kOutput, calls=%fused_computation.44.clone.1 | convolution fusion | flops 1705525248 | bytes 17467008 | tf_op jit(solution)/shard_map/while/body/eval_jaxpr/kgtn,nkd->kgtd/dot_general | solution.py:97
  996.7 7.9 fusion.80
  1004.6 12.0 %fusion.81 = f32[2,8,128,128]{3,2,1,0:T(8,128)S(1)} fusion(f32[2,1601,128,8]{2,1,3,0:T(8,128)} %fusion.80, bf16[2,8,128,128]{3,2,1,0:T(8,128)(2,1)S(1)} %get-tuple-element.1009, f32[2,8,128]{2,1,0:T(8,128)S(1)} %get-tuple-element.1010, f32[2,8,128]{2,1,0:T(8,128)S(1)} %get-tuple-element.1007, f32[2,8,128]{2,1,0:T(8,128)S(1)} %get-tuple-element.1006, ...), kind=kOutput, calls=%fused_computation.44.clone.1 | convolution fusion | flops 1705525248 | bytes 17467008 | tf_op jit(solution)/shard_map/while/body/eval_jaxpr/kgtn,nkd->kgtd/dot_general | solution.py:97
  1022.8 43.0 %all-gather.2.cloned.1.call-done = bf16[512,2048]{0,1:T(8,128)(2,1)} async-done(((bf16[128,2048]{0,1:T(8,128)(2,1)}), bf16[512,2048]{0,1:T(8,128)(2,1)}) %all-gather.2.cloned.1.call-update) | async-done | bytes 2097168 | tf_op jit(solution)/shard_map/all_gather | solution.py:167
  1065.8 18.1 %fusion.42 = f32[2048,2048]{0,1:T(8,128)} fusion(bf16[512,2048]{0,1:T(8,128)(2,1)} %all-gather.2.cloned.1.call-done, bf16[512,2048]{1,0:T(8,128)(2,1)S(1)} %bitcast.154, f32[2048]{0:T(1024)S(1)} %copy-done.9, f32[2048,2048]{0,1:T(8,128)} %copy.78), kind=kOutput, calls=%fused_computation.61 | convolution fusion | flops 4357881856 | bytes 37756928 | tf_op jit(solution)/shard_map/dot_general | solution.py:165
  1083.9 17.6 %copy.96 = f32[2048,2048]{1,0:T(8,128)} copy(f32[2048,2048]{0,1:T(8,128)} %fusion.42) | data formatting | bytes 33554432 | tf_op jit(solution)/shard_map/mul | solution.py:173
  (147 shorter events, 157.9 us)
Async XLA Ops:
  24.1 12.4 %copy-start.8 = (f32[2048]{0:T(1024)S(1)}, f32[2048]{0:T(1024)}, u32[]{:S(2)}) copy-start(f32[2048]{0:T(1024)} %param.16) | copy-start | bytes 24580
  36.5 200.6 %copy-start.1 = (bf16[128,8192]{1,0:T(8,128)(2,1)S(1)}, bf16[128,8192]{1,0:T(8,128)(2,1)}, u32[]{:S(2)}) copy-start(bf16[128,8192]{1,0:T(8,128)(2,1)} %param.13) | copy-start | bytes 6291460
  50.4 371.0 %copy-start.11 = (s32[3]{0:T(128)S(1)}, s32[3]{0:T(128)}, u32[]{:S(2)}) copy-start(s32[3]{0:T(128)} %param.20) | copy-start | bytes 40
  50.4 186.7 %collective-permute-start = (bf16[2048,2048]{0,1:T(8,128)(2,1)}, bf16[2048,2048]{0,1:T(8,128)(2,1)}, u32[]{:S(2)}, u32[]{:S(2)}) collective-permute-start(bf16[2048,2048]{0,1:T(8,128)(2,1)} %multiply_convert_fusion), channel_id=1, source_target_pairs={{0,4},{4,8},{8,12},{12,0},{1,5},{5,9},{9,13},{13,1},{2,6},{6,10},{... | collective-permute-start | bytes 25165832 | tf_op jit(solution)/shard_map/ppermute | solution.py:136
  53.5 386.7 %collective-permute-start.2 = (bf16[2048,2048]{0,1:T(8,128)(2,1)}, bf16[2048,2048]{0,1:T(8,128)(2,1)}, u32[]{:S(2)}, u32[]{:S(2)}) collective-permute-start(bf16[2048,2048]{0,1:T(8,128)(2,1)} %multiply_convert_fusion), channel_id=1, source_target_pairs={{4,0},{8,4},{12,8},{0,12},{5,1},{9,5},{13,9},{1,13},{6,2},{10,6},{... | collective-permute-start | bytes 25165832 | tf_op jit(solution)/shard_map/ppermute | solution.py:140
  237.1 361.5 %collective-permute-start.1 = (bf16[2048,2048]{0,1:T(8,128)(2,1)}, bf16[2048,2048]{0,1:T(8,128)(2,1)}, u32[]{:S(2)}, u32[]{:S(2)}) collective-permute-start(bf16[2048,2048]{0,1:T(8,128)(2,1)} %collective-permute-done), channel_id=1, source_target_pairs={{0,4},{4,8},{8,12},{12,0},{1,5},{5,9},{9,13},{13,1},{2,6},{6,10},{... | collective-permute-start | bytes 25165832 | tf_op jit(solution)/shard_map/ppermute | solution.py:136
  239.6 780.3 %all-to-all-start = ((bf16[128,4,2048]{0,2,1:T(8,128)(2,1)}), bf16[128,4,2048]{0,2,1:T(8,128)(2,1)}, u32[]{:S(2)}, u32[]{:S(2)}) async-start(bf16[128,4,2048]{0,2,1:T(8,128)(2,1)} %bitcast.16), calls=%async_computation | async-start | bytes 4194304 | tf_op jit(solution)/shard_map/all_to_all | solution.py:126
  421.1 644.7 %all-gather.2.cloned.1.call-start = ((), (), s32[]{:S(2)}) async-start(), calls=%async_computation.1 | async-start | bytes 2621440 | tf_op jit(solution)/shard_map/all_gather | solution.py:167
  429.5 10.3 copy-start.10
  801.3 23.0 %copy-start.2 = (bf16[128,8192]{1,0:T(8,128)(2,1)S(1)}, bf16[128,8192]{1,0:T(8,128)(2,1)}, u32[]{:S(2)}) copy-start(bf16[128,8192]{1,0:T(8,128)(2,1)} %param.13) | copy-start | bytes 6291460
  824.3 17.9 %copy-start.5 = (f32[2,8,128,128]{3,2,1,0:T(8,128)S(1)}, f32[2,8,128,128]{3,2,1,0:T(8,128)}, u32[]{:S(2)}) copy-start(f32[2,8,128,128]{3,2,1,0:T(8,128)} %custom-call.2) | copy-start | bytes 3145732
  824.3 17.9 %copy-start.6 = (f32[2,8,128]{2,1,0:T(8,128)S(1)}, f32[2,8,128]{2,1,0:T(8,128)}, u32[]{:S(2)}) copy-start(f32[2,8,128]{2,1,0:T(8,128)} %custom-call) | copy-start | bytes 24580
  824.3 17.9 %copy-start.7 = (f32[2,8,128]{2,1,0:T(8,128)S(1)}, f32[2,8,128]{2,1,0:T(8,128)}, u32[]{:S(2)}) copy-start(f32[2,8,128]{2,1,0:T(8,128)} %custom-call.1) | copy-start | bytes 24580
  842.2 91.2 %copy-start = (bf16[128,2048]{0,1:T(8,128)(2,1)S(1)}, bf16[128,2048]{0,1:T(8,128)(2,1)}, u32[]{:S(2)}) copy-start(bf16[128,2048]{0,1:T(8,128)(2,1)} %copy.88) | copy-start | bytes 1572868
  934.0 131.8 %copy-start.9 = (f32[2048]{0:T(1024)S(1)}, f32[2048]{0:T(1024)}, u32[]{:S(2)}) copy-start(f32[2048]{0:T(1024)} %param.16) | copy-start | bytes 24580
  934.1 7.9 copy-start.3
  954.0 1.0 copy-start.4
  955.0 7.9 copy-start.3
  974.9 1.0 copy-start.4
  975.8 7.9 copy-start.3
  995.7 1.0 copy-start.4
  996.7 7.9 copy-start.3
  1016.6 1.0 copy-start.4
Sparse Core Ops, SparseCore 0:
  1020.0 45.7 all-gather.1
